TPU v7x, 32 devices: a whole 2x2x4 slice. The times are simulated.
32 devices in a mesh: groups: 2 (over y), seq: 4 (over z), cell: 4 (over x, core).
Axes of the slice: x: 2, y: 2, z: 4, core: 2. Of those that a mesh axis runs over, the one named last changes fastest.
Arguments:
- dna_bases: int32 [65536], P(('groups', 'seq')), parts along dimension 0, may hold values from 0 to 3
- stem_weight: bfloat16 [512, 768], replicated, may hold values from -0.5 to 0.5
- conv_weight: bfloat16 [2, 384, 3, 768], P(None, 'cell'), may hold values from -0.125 to 0.125
- proj_weight: bfloat16 [2, 384, 768], P(None, 'cell'), may hold values from -0.3125 to 0.3125
- emission_head_weight: bfloat16 [32, 768, 128], P('cell'), may hold values from -0.046875 to 0.046875
- transitions: float32 [32, 128, 128], P('cell'), may hold values from -1 to 109
Outputs:
- log_marginals: float32 [32, 512, 128], P('cell', ('groups', 'seq')), parts along dimension 1
There are 2 independent parts, one for each index of `groups`. A program takes and returns all parts, laid end to end along the dimension named above; an argument that names none is the same for every part. Nothing has to cross between parts.
All inputs are finite; a program needn't handle non-finite values.
Results may differ from a plain program's by a relative error of at most 0.0007.
Values may be sent and summed in bfloat16 or wider, within the bound.
A program may use at most 128 MiB of HBM per device.

v0:
```python
import jax
import jax.numpy as jnp
from jax import lax
from jax.sharding import PartitionSpec as P

BIN_BP = 128
BASE_DILATION = 4


def with_halo(block, sides, width):
    for axis, dim in sides:
        count = lax.axis_size(axis)
        forward = [(i, i + 1) for i in range(count - 1)]
        backward = [(target, source) for source, target in forward]
        low = lax.ppermute(
            lax.slice_in_dim(block, block.shape[dim] - width, None, axis=dim), axis, forward
        )
        high = lax.ppermute(lax.slice_in_dim(block, 0, width, axis=dim), axis, backward)
        block = jnp.concatenate([low, block, high], axis=dim)
    return block


def prefix(value, axis, join, neutral, backward):
    count = lax.axis_size(axis)
    place = lax.axis_index(axis)
    ahead = count - 1 - place if backward else place
    gathered = lax.all_gather(value.astype(jnp.bfloat16), axis)
    state = jnp.zeros_like(value) + jnp.asarray(neutral, value.dtype)

    def one(lap, state):
        source = count - 1 - lap if backward else lap
        return join(state, lax.dynamic_index_in_dim(gathered, source, 0, False).astype(value.dtype))

    return lax.fori_loop(0, ahead, one, state)


def scaled(values):
    return values * lax.rsqrt(jnp.mean(values * values, axis=-1, keepdims=True) + 1e-06)


def tap_stack(conv_input, spacing_multiplier):
    out_rows = conv_input.shape[0] - 2 * spacing_multiplier
    return jnp.concatenate(
        [
            conv_input[0:out_rows],
            conv_input[spacing_multiplier : spacing_multiplier + out_rows],
            conv_input[2 * spacing_multiplier : 2 * spacing_multiplier + out_rows],
        ],
        axis=1,
    )


def mat_prod(left_mat, trailing_product):
    return jnp.einsum("crs,cst->crt", left_mat, trailing_product, precision=lax.Precision.HIGHEST)


def unit_peak(matrix):
    return matrix / jnp.max(matrix, axis=(-2, -1), keepdims=True)


def vec_peak(vector):
    return vector / jnp.max(vector, axis=-1, keepdims=True)


def forward_join(early_mat, late_mat):
    return unit_peak(mat_prod(early_mat, late_mat))


def backward_join(early_mat, late_mat):
    return unit_peak(mat_prod(late_mat, early_mat))


def branch(stacked, conv_slice, proj_slice):
    flat_weight = conv_slice.reshape(conv_slice.shape[0], -1)
    conv_out = lax.dot_general(
        stacked, flat_weight, (((1,), (1,)), ((), ())), preferred_element_type=jnp.float32
    )
    hidden = jax.nn.gelu(conv_out).astype(jnp.bfloat16)
    partial_value = jnp.dot(hidden, proj_slice, preferred_element_type=jnp.float32)
    return lax.psum(partial_value.astype(jnp.bfloat16), "cell").astype(jnp.float32)


def per_device(dna_bases, stem_weight, conv_weight, proj_weight, emission_head_weight, transitions):
    bin_rows = dna_bases.shape[0] // BIN_BP
    base_hits = dna_bases.reshape(bin_rows, BIN_BP, 1) == jnp.arange(4, dtype=jnp.int32)
    one_hot = base_hits.astype(jnp.bfloat16).reshape(bin_rows, BIN_BP * 4)
    stem_out = jnp.dot(one_hot, stem_weight, preferred_element_type=jnp.float32).astype(
        jnp.bfloat16
    )
    layers = conv_weight.shape[0]
    residual = stem_out.astype(jnp.float32)
    for layer_position in range(layers):
        spacing_multiplier = BASE_DILATION * 2**layer_position
        conv_input = jax.nn.gelu(scaled(residual)).astype(jnp.bfloat16)
        widened = with_halo(conv_input, (("seq", 0),), spacing_multiplier)
        residual = residual + branch(
            tap_stack(widened, spacing_multiplier),
            conv_weight[layer_position],
            proj_weight[layer_position],
        )
    trunk_features = scaled(residual).astype(jnp.bfloat16)
    emission_scores = jnp.einsum(
        "td,cds->cts", trunk_features, emission_head_weight, preferred_element_type=jnp.float32
    )
    cell_count = emission_scores.shape[0]
    state_count = emission_scores.shape[2]
    scaling = jnp.exp(emission_scores - jnp.max(emission_scores, axis=2, keepdims=True))
    trans_exp = jnp.exp(transitions - jnp.max(transitions, axis=(1, 2), keepdims=True))
    sub_len = 8
    sub_count = bin_rows // sub_len
    factors = scaling.reshape(cell_count, sub_count, sub_len, state_count)

    def block_product(inputs):
        transition_matrix, factor = inputs
        running_state = transition_matrix[None] * factor[:, 0, None, :]
        for position in range(1, sub_len):
            running_state = (
                jnp.einsum(
                    "ylv,vu->ylu", running_state, transition_matrix, precision=lax.Precision.HIGHEST
                )
                * factor[:, position, None, :]
            )
            running_state = unit_peak(running_state)
        combined = running_state
        for level_index in range(sub_count.bit_length() - 1):
            half_count = combined.shape[0] // 2
            paired_states = combined.reshape(half_count, 2, state_count, state_count)
            combined = unit_peak(
                jnp.einsum(
                    "mpw,mwy->mpy",
                    paired_states[:, 0],
                    paired_states[:, 1],
                    precision=lax.Precision.HIGHEST,
                )
            )
        return (running_state, combined[0])

    segment_list, block = lax.map(block_product, (trans_exp, factors))
    identity = jnp.broadcast_to(jnp.eye(state_count, dtype=jnp.float32), block.shape)
    prefix_mat = prefix(block, "seq", forward_join, identity, False)
    suffix_mat = prefix(block, "seq", backward_join, identity, True)
    enter_vec = vec_peak(jnp.sum(prefix_mat, axis=1))
    leave_vec = vec_peak(jnp.sum(suffix_mat, axis=2))
    chain_pieces = jnp.swapaxes(segment_list, 0, 1)

    def forward_step(vector, piece_mat):
        return (
            vec_peak(jnp.einsum("cr,crs->cs", vector, piece_mat, precision=lax.Precision.HIGHEST)),
            vector,
        )

    def backward_step(vector, piece_mat):
        return (
            vec_peak(jnp.einsum("crs,cs->cr", piece_mat, vector, precision=lax.Precision.HIGHEST)),
            vector,
        )

    _, starts = lax.scan(forward_step, enter_vec, chain_pieces)
    _, after_vecs = lax.scan(backward_step, leave_vec, chain_pieces, reverse=True)
    vector = jnp.swapaxes(starts, 0, 1)
    forward_list = []
    for position in range(sub_len):
        vector = vec_peak(
            jnp.einsum("cgr,crs->cgs", vector, trans_exp, precision=lax.Precision.HIGHEST)
            * factors[:, :, position]
        )
        forward_list.append(vector)
    vector = jnp.swapaxes(after_vecs, 0, 1)
    backward_list = [vector] * sub_len
    for position in range(sub_len - 1, -1, -1):
        backward_list[position] = vector
        if position > 0:
            vector = vec_peak(
                jnp.einsum(
                    "crs,cgs->cgr",
                    trans_exp,
                    factors[:, :, position] * vector,
                    precision=lax.Precision.HIGHEST,
                )
            )
    alpha_all = jnp.stack(forward_list, axis=2).reshape(cell_count, bin_rows, state_count)
    beta_all = jnp.stack(backward_list, axis=2).reshape(cell_count, bin_rows, state_count)
    joint_log = jnp.log(alpha_all) + jnp.log(beta_all)
    return jnp.maximum(joint_log - jax.nn.logsumexp(joint_log, axis=2, keepdims=True), -30.0)


def solution(mesh):
    placed = (
        P(("groups", "seq")),
        P(),
        P(None, "cell", None, None),
        P(None, "cell", None),
        P("cell", None, None),
        P("cell", None, None),
    )
    return jax.shard_map(
        per_device,
        mesh=mesh,
        in_specs=placed,
        out_specs=P("cell", ("groups", "seq"), None),
        check_vma=False,
    )
```

profile of v0, /device:TPU:0, one launch (start us, length us, event | category | flops | bytes accessed | tf_op | source)
XLA Modules:
  0.0 269.2 jit_solution(5592147471232159884)
XLA Ops:
  7.7 1.7 multiply_reduce_fusion.2
  9.5 5.0 %collective-permute-start = (bf16[4,768]{1,0:T(4,128)(2,1)S(1)}, bf16[4,768]{1,0:T(4,128)(2,1)S(1)}, u32[]{:S(2)}, u32[]{:S(2)}) collective-permute-start(bf16[4,768]{1,0:T(4,128)(2,1)S(1)} %get-tuple-element.359), channel_id=1, source_target_pairs={{0,4},{4,8},{8,12},{1,5},{5,9},{9,13},{2,6},{6,10},{10,14},{3,7},{... | collective-permute-start | bytes 18440 | tf_op jit(solution)/shard_map/ppermute | solution.py:15
  17.6 2.6 collective-permute-done.1
  20.2 2.0 convolution_convert_fusion.2
  22.3 32.0 %all-reduce.3.cloned.1.call-done = bf16[64,768]{1,0:T(8,128)(2,1)} async-done(((bf16[64,768]{1,0:T(8,128)(2,1)}), bf16[64,768]{1,0:T(8,128)(2,1)}) %all-reduce.3.cloned.1.call-update) | async-done | bytes 98320 | tf_op jit(solution)/shard_map/psum | solution.py:80
  56.5 3.4 %collective-permute-start.2 = (bf16[8,768]{1,0:T(8,128)(2,1)S(1)}, bf16[8,768]{1,0:T(8,128)(2,1)S(1)}, u32[]{:S(2)}, u32[]{:S(2)}) collective-permute-start(bf16[8,768]{1,0:T(8,128)(2,1)S(1)} %get-tuple-element.357), channel_id=1, source_target_pairs={{0,4},{4,8},{8,12},{1,5},{5,9},{9,13},{2,6},{6,10},{10,14},{3,7},{... | collective-permute-start | bytes 36872 | tf_op jit(solution)/shard_map/ppermute | solution.py:15
  61.8 3.7 %collective-permute-done.3 = bf16[8,768]{1,0:T(8,128)(2,1)S(1)} collective-permute-done((bf16[8,768]{1,0:T(8,128)(2,1)S(1)}, bf16[8,768]{1,0:T(8,128)(2,1)S(1)}, u32[]{:S(2)}, u32[]{:S(2)}) %collective-permute-start.3) | collective-permute-done | bytes 12320 | tf_op jit(solution)/shard_map/ppermute | solution.py:18
  65.5 2.0 convolution_convert_fusion.1
  67.7 30.7 %all-reduce.5.cloned.1.call-done = bf16[64,768]{1,0:T(8,128)(2,1)} async-done(((bf16[64,768]{1,0:T(8,128)(2,1)}), bf16[64,768]{1,0:T(8,128)(2,1)}) %all-reduce.5.cloned.1.call-update) | async-done | bytes 98320 | tf_op jit(solution)/shard_map/psum | solution.py:80
  100.9 73.1 %while.62 = (s32[]{:T(128)}, f32[8,8,128,128]{3,2,0,1:T(8,128)}, bf16[8,128,128]{2,1,0:T(8,128)(2,1)}, f32[8,128,128]{2,1,0:T(8,128)S(1)}, f32[8,8,8,128]{3,2,1,0:T(8,128)S(1)}, /*index=5*/s32[]{:T(128)}) while((s32[]{:T(128)}, f32[8,8,128,128]{3,2,0,1:T(8,128)}, bf16[8,128,128]{2,1,0:T(8,128)(2,1)}, f32[8,128,128]{2,1,0:T(8,128)S(1)}, ...), condition=%wide.region_18.19_spmd, body=%wide.region_7.18_spmd.sunk | while | flops 1588559872 | bytes 11572125 | solution.py:138
  174.3 27.8 %all-gather.3.cloned.1.call-done = bf16[32,128,128]{2,1,0:T(8,128)(2,1)} async-done(((bf16[8,128,128]{2,1,0:T(8,128)(2,1)}), bf16[32,128,128]{2,1,0:T(8,128)(2,1)}) %all-gather.3.cloned.1.call-update) | async-done | bytes 1048592 | tf_op jit(solution)/shard_map/all_gather | solution.py:27
  202.6 14.4 %while.64 = (s32[]{:T(128)}, f32[8,128]{1,0:T(8,128)S(1)}, f32[8,8,128]{2,1,0:T(8,128)S(1)}, f32[8,8,128,128]{3,2,1,0:T(8,128)}, s32[]{:T(128)}, /*index=5*/f32[]{:T(128)}) while((s32[]{:T(128)}, f32[8,128]{1,0:T(8,128)S(1)}, f32[8,8,128]{2,1,0:T(8,128)S(1)}, f32[8,8,128,128]{3,2,1,0:T(8,128)}, s32[]{:T(128)}, /*index=5*/f32[]{:T(128)}) %tuple.192), condition=%wide.region_26.27_spmd, body=%wide.region_24.26_spmd.sunk | while | flops 1574906 | bytes 553613 | solution.py:158
  202.6 1.6 fusion.296
  206.2 1.6 fusion.296
  218.3 5.0 %while.65 = (s32[]{:T(128)}, f32[8,128,128]{2,1,0:T(8,128)S(1)}, s32[]{:T(128)}, bf16[4,8,128,128]{3,2,1,0:T(8,128)(2,1)}, s32[]{:T(128)}, /*index=5*/s32[]{:T(128)}, s32[]{:T(128)}, s32[]{:T(128)}) while((s32[]{:T(128)}, f32[8,128,128]{2,1,0:T(8,128)S(1)}, s32[]{:T(128)}, bf16[4,8,128,128]{3,2,1,0:T(8,128)(2,1)}, s32[]{:T(128)}, ...), condition=%wide.region_37.38_spmd, body=%wide.region_35.37_spmd.sunk | while | flops 201588736 | bytes 2359495 | solution.py:34
  223.7 17.6 %while.66 = (s32[]{:T(128)}, f32[8,128]{1,0:T(8,128)S(1)}, f32[8,8,128]{2,0,1:T(8,128)S(1)}, f32[8,8,128,128]{3,2,1,0:T(8,128)}, s32[]{:T(128)}, /*index=5*/s32[]{:T(128)}, f32[]{:T(128)}, s32[]{:T(128)}) while((s32[]{:T(128)}, f32[8,128]{1,0:T(8,128)S(1)}, f32[8,8,128]{2,0,1:T(8,128)S(1)}, f32[8,8,128,128]{3,2,1,0:T(8,128)}, s32[]{:T(128)}, ...), condition=%wide.region_42.43_spmd, body=%wide.region_40.42_spmd.sunk | while | flops 1574907 | bytes 553133 | solution.py:159
  223.7 2.0 fusion.301
  225.9 2.0 fusion.301
  228.1 2.0 fusion.301
  230.3 2.0 fusion.301
  232.5 2.0 fusion.301
  234.7 2.0 fusion.301
  236.9 2.0 fusion.301
  239.1 2.0 fusion.301
  (304 shorter events, 125.2 us)
Async XLA Ops:
  6.5 92.9 %copy-start = (bf16[8,768,128]{2,1,0:T(8,128)(2,1)S(1)}, bf16[8,768,128]{2,1,0:T(8,128)(2,1)}, u32[]{:S(2)}) copy-start(bf16[8,768,128]{2,1,0:T(8,128)(2,1)} %param.20) | copy-start | bytes 4718596
  6.5 47.8 %all-reduce.3.cloned.1.call-start = ((), (), s32[]{:S(2)}) async-start(), calls=%async_computation | async-start | bytes 196608 | tf_op jit(solution)/shard_map/psum | solution.py:80
  9.5 8.1 %collective-permute-start = (bf16[4,768]{1,0:T(4,128)(2,1)S(1)}, bf16[4,768]{1,0:T(4,128)(2,1)S(1)}, u32[]{:S(2)}, u32[]{:S(2)}) collective-permute-start(bf16[4,768]{1,0:T(4,128)(2,1)S(1)} %get-tuple-element.359), channel_id=1, source_target_pairs={{0,4},{4,8},{8,12},{1,5},{5,9},{9,13},{2,6},{6,10},{10,14},{3,7},{... | collective-permute-start | bytes 18440 | tf_op jit(solution)/shard_map/ppermute | solution.py:15
  14.5 47.1 %copy-start.1 = (f32[8,128,128]{2,1,0:T(8,128)S(1)}, f32[8,128,128]{2,1,0:T(8,128)}, u32[]{:S(2)}) copy-start(f32[8,128,128]{2,1,0:T(8,128)} %param.21) | copy-start | bytes 1572868
  14.5 5.7 %collective-permute-start.1 = (bf16[4,768]{1,0:T(4,128)(2,1)S(1)}, bf16[4,768]{1,0:T(4,128)(2,1)S(1)}, u32[]{:S(2)}, u32[]{:S(2)}) collective-permute-start(bf16[4,768]{1,0:T(4,128)(2,1)S(1)} %get-tuple-element.360), channel_id=1, source_target_pairs={{4,0},{8,4},{12,8},{5,1},{9,5},{13,9},{6,2},{10,6},{14,10},{7,3},{... | collective-permute-start | bytes 18440 | tf_op jit(solution)/shard_map/ppermute | solution.py:18
  22.2 76.2 %all-reduce.5.cloned.1.call-start = ((), (), s32[]{:S(2)}) async-start(), calls=%async_computation.1 | async-start | bytes 196608 | tf_op jit(solution)/shard_map/psum | solution.py:80
  54.3 44.1 %copy-start.2 = (bf16[64,768]{1,0:T(8,128)(2,1)S(1)}, bf16[64,768]{1,0:T(8,128)(2,1)}, u32[]{:S(2)}) copy-start(bf16[64,768]{1,0:T(8,128)(2,1)} %all-reduce.3.cloned.1.call-done) | copy-start | bytes 294916
  56.5 5.3 %collective-permute-start.2 = (bf16[8,768]{1,0:T(8,128)(2,1)S(1)}, bf16[8,768]{1,0:T(8,128)(2,1)S(1)}, u32[]{:S(2)}, u32[]{:S(2)}) collective-permute-start(bf16[8,768]{1,0:T(8,128)(2,1)S(1)} %get-tuple-element.357), channel_id=1, source_target_pairs={{0,4},{4,8},{8,12},{1,5},{5,9},{9,13},{2,6},{6,10},{10,14},{3,7},{... | collective-permute-start | bytes 36872 | tf_op jit(solution)/shard_map/ppermute | solution.py:15
  59.9 5.6 %collective-permute-start.3 = (bf16[8,768]{1,0:T(8,128)(2,1)S(1)}, bf16[8,768]{1,0:T(8,128)(2,1)S(1)}, u32[]{:S(2)}, u32[]{:S(2)}) collective-permute-start(bf16[8,768]{1,0:T(8,128)(2,1)S(1)} %get-tuple-element.358), channel_id=1, source_target_pairs={{4,0},{8,4},{12,8},{5,1},{9,5},{13,9},{6,2},{10,6},{14,10},{7,3},{... | collective-permute-start | bytes 36872 | tf_op jit(solution)/shard_map/ppermute | solution.py:18
  67.5 134.7 %all-gather.3.cloned.1.call-start = ((), (), s32[]{:S(2)}) async-start(), calls=%async_computation.2 | async-start | bytes 1310720 | tf_op jit(solution)/shard_map/all_gather | solution.py:27
Sparse Core Ops, SparseCore 0:
  22.4 31.9 all-reduce.2
  67.6 30.7 all-reduce.4
  174.1 27.9 all-gather.2
where the time goes:
time: 271 us; the launch traced here: 269 us
  matrix products  104 us (38%)
  waiting for transfers between devices  96.8 us (36%)
  other arithmetic  37.8 us (14%)
  between operations  13.5 us (5%)
  starting transfers between devices  11.1 us (4%)
  local copies, waits for them, and re-layouts  4.66 us (2%)
    psum x2, waiting for transfers between devices, branch(): lax.psum(partial_value.astype(jnp.bfloat16), 'cell').astype(jnp.float32)  62.7 us
    dot_general x56, matrix products, block_product(): jnp.einsum('ylv,vu->ylu', running_state, transition_matrix, precision=lax...  40 us
    all_gather x1, waiting for transfers between devices, prefix(): gathered = lax.all_gather(value.astype(jnp.bfloat16), axis)  27.8 us
    dynamic_update_slice x16, other arithmetic, per_device(): segment_list, block = lax.map(block_product, (trans_exp, factors))  17.7 us
    dot_general x8, matrix products, backward_step(): jnp.einsum('crs,cs->cr', piece_mat, vector, precision=lax.Precision.HIGHEST)  15.7 us
    dot_general x24, matrix products, block_product(): jnp.einsum('mpw,mwy->mpy', paired_states[:, 0], paired_states[:, 1], prec...  13.3 us
    dot_general x8, matrix products, forward_step(): jnp.einsum('cr,crs->cs', vector, piece_mat, precision=lax.Precision.HIGHEST)  12.8 us
    div x33, other arithmetic, vec_peak(): return vector / jnp.max(vector, axis=-1, keepdims=True)  10.7 us
  transfers between devices with their start and end apart: 7, of which 5 were waited for; matrix products, arithmetic and copies ran while one was open for 1% of the time, Pallas kernels for 0%

commit v1 on v0

v1 whole, which is shorter than its diff:
```python
import functools

import jax
import jax.numpy as jnp
from jax import lax
from jax.experimental import pallas as pl
from jax.experimental.pallas import tpu as pltpu
from jax.sharding import PartitionSpec as P

BIN_BP = 128
BASE_DILATION = 4
SUB = 8
MESH = pl.DeviceIdType.MESH
F32 = jnp.float32
BF16 = jnp.bfloat16


def halves(x):
    hi = x.astype(BF16).astype(F32)
    return hi, x - hi


def beside(x):
    hi, lo = halves(x)
    return jnp.concatenate([hi.astype(BF16), lo.astype(BF16)], axis=1)


def above(x):
    hi, lo = halves(x)
    return jnp.concatenate([hi, lo], axis=0).astype(BF16)


def row_times(stacked, pair):
    n = pair.shape[1] // 2
    y = jnp.dot(stacked, pair, preferred_element_type=F32)
    y = y[:, :n] + y[:, n:]
    half = y.shape[0] // 2
    return y[:half] + y[half:]


def row_times_t(stacked, pair):
    y = lax.dot_general(
        jnp.concatenate([stacked, stacked], axis=1),
        pair,
        (((1,), (1,)), ((), ())),
        preferred_element_type=F32,
    )
    half = y.shape[0] // 2
    return y[:half] + y[half:]


def unit_rows(v):
    return v / jnp.max(v, axis=-1, keepdims=True)


def top(x):
    return jnp.max(jnp.max(x, axis=-1, keepdims=True), axis=-2, keepdims=True)


def crf_kernel(
    feat_ref, head_ref, trans_ref, out_ref,
    f_ref, pair_ref, flip_ref, tree_ref, vin, win, vgot, wgot, vout, wout, st_ref, af_ref,
    al_ref, be_ref, ssem, rsem,
):
    cells, states = head_ref.shape[0], head_ref.shape[2]
    bins = feat_ref.shape[0]
    count = bins // SUB
    n = lax.axis_size("seq")
    me = lax.axis_index("seq")

    if n > 1:
        barrier = pltpu.get_barrier_semaphore()

        @pl.when(me > 0)
        def _():
            pl.semaphore_signal(barrier, inc=1, device_id={"seq": me - 1}, device_id_type=MESH)

        @pl.when(me < n - 1)
        def _():
            pl.semaphore_signal(barrier, inc=1, device_id={"seq": me + 1}, device_id_type=MESH)

        inner = jnp.logical_and(me > 0, me < n - 1)
        pl.semaphore_wait(barrier, jnp.where(inner, 2, 1))

    def chain(c, _):
        scores = jnp.dot(feat_ref[...], head_ref[c], preferred_element_type=F32)
        f_ref[c] = jnp.exp(scores - jnp.max(scores, axis=1, keepdims=True))
        raw = trans_ref[c]
        t = jnp.exp(raw - top(raw))
        pair = beside(t)
        pair_ref[c] = pair
        flip_ref[c] = beside(t.T)
        twice = jnp.concatenate([pair, pair], axis=0)
        x = t[None] * f_ref[c, pl.ds(0, count, stride=SUB), :][:, None, :]
        for j in range(1, SUB):
            scale = 1.0 / top(x)
            g = f_ref[c, pl.ds(j, count, stride=SUB), :][:, None, :] * scale
            y = jnp.dot(
                beside(x.reshape(count * states, states)), twice, preferred_element_type=F32
            )
            x = (y[:, :states] + y[:, states:]).reshape(count, states, states) * g
        x = x * (1.0 / top(x))
        nodes = []
        for k in range(count):
            nodes.append(beside(x[k]))
            tree_ref[c, k] = nodes[k]
        place = count
        while len(nodes) > 1:
            joined = []
            for k in range(0, len(nodes), 2):
                right = jnp.concatenate([nodes[k + 1], nodes[k + 1]], axis=0)
                y = jnp.dot(nodes[k], right, preferred_element_type=F32)
                y = y[:, :states] + y[:, states:]
                node = beside(y * (1.0 / top(y)))
                tree_ref[c, place] = node
                place += 1
                joined.append(node)
            nodes = joined
        return 0

    lax.fori_loop(0, cells, chain, 0)

    rows = lax.broadcasted_iota(jnp.int32, (cells, states), 0)

    def through(v, node, times):
        stacked = above(v)
        out = jnp.zeros_like(v)
        for c in range(cells):
            out = jnp.where(rows == c, times(stacked, tree_ref[c, node]), out)
        return unit_rows(out)

    whole = 2 * count - 2

    def forward_carry():
        @pl.when(me == 0)
        def _():
            vin[...] = jnp.ones_like(vin)

        @pl.when(me > 0)
        def _():
            pltpu.make_async_remote_copy(
                vout, vgot, ssem.at[0], rsem.at[0], device_id={"seq": me - 1}, device_id_type=MESH
            ).wait_recv()
            vin[...] = vgot[...]

        @pl.when(me < n - 1)
        def _():
            vout[...] = through(vin[...], whole, row_times)
            pltpu.make_async_remote_copy(
                vout, vgot, ssem.at[0], rsem.at[0], device_id={"seq": me + 1}, device_id_type=MESH
            ).start()

    def backward_carry():
        @pl.when(me == n - 1)
        def _():
            win[...] = jnp.ones_like(win)

        @pl.when(me < n - 1)
        def _():
            pltpu.make_async_remote_copy(
                wout, wgot, ssem.at[1], rsem.at[1], device_id={"seq": me + 1}, device_id_type=MESH
            ).wait_recv()
            win[...] = wgot[...]

        @pl.when(me > 0)
        def _():
            wout[...] = through(win[...], whole, row_times_t)
            pltpu.make_async_remote_copy(
                wout, wgot, ssem.at[1], rsem.at[1], device_id={"seq": me - 1}, device_id_type=MESH
            ).start()

    if n > 1:
        @pl.when(2 * me < n)
        def _():
            forward_carry()
            backward_carry()

        @pl.when(2 * me >= n)
        def _():
            backward_carry()
            forward_carry()
    else:
        vin[...] = jnp.ones_like(vin)
        win[...] = jnp.ones_like(win)

    starts = {0: vin[...]}
    afters = {count - 1: win[...]}
    width = count // 2
    base = 2 * count - 4
    while width >= 1:
        for k in range(0, count, 2 * width):
            starts[k + width] = through(starts[k], base + k // width, row_times)
            end = k + 2 * width - 1
            afters[end - width] = through(afters[end], base + end // width, row_times_t)
        width //= 2
        if width:
            base -= count // width
    for k in range(count):
        st_ref[pl.ds(k * cells, cells), :] = starts[k]
        af_ref[pl.ds(k * cells, cells), :] = afters[k]

    ahead = [st_ref[pl.ds(c, count, stride=cells), :] for c in range(cells)]
    behind = [af_ref[pl.ds(c, count, stride=cells), :] for c in range(cells)]
    for j in range(SUB):
        i = SUB - 1 - j
        for c in range(cells):
            fj = f_ref[c, pl.ds(j, count, stride=SUB), :]
            v = row_times(above(ahead[c]), pair_ref[c]) * fj
            v = unit_rows(v)
            al_ref[c, pl.ds(j * count, count), :] = v
            ahead[c] = v
            be_ref[c, pl.ds(i * count, count), :] = behind[c]
            if i > 0:
                fi = f_ref[c, pl.ds(i, count, stride=SUB), :]
                behind[c] = unit_rows(row_times(above(behind[c] * fi), flip_ref[c]))
    for c in range(cells):
        joint = jnp.log(al_ref[c]) + jnp.log(be_ref[c])
        peak = jnp.max(joint, axis=1, keepdims=True)
        total = jnp.log(jnp.sum(jnp.exp(joint - peak), axis=1, keepdims=True))
        result = jnp.maximum(joint - peak - total, -30.0)
        for j in range(SUB):
            out_ref[c, pl.ds(j, count, stride=SUB), :] = result[j * count : (j + 1) * count]

    if n > 1:
        @pl.when(me < n - 1)
        def _():
            pltpu.make_async_remote_copy(
                vout, vgot, ssem.at[0], rsem.at[0], device_id={"seq": me + 1}, device_id_type=MESH
            ).wait_send()

        @pl.when(me > 0)
        def _():
            pltpu.make_async_remote_copy(
                wout, wgot, ssem.at[1], rsem.at[1], device_id={"seq": me - 1}, device_id_type=MESH
            ).wait_send()


def crf(features, heads, transitions):
    bins = features.shape[0]
    cells, _, states = heads.shape
    count = bins // SUB
    vmem = pl.BlockSpec(memory_space=pltpu.VMEM)
    vec = pltpu.VMEM((cells, states), F32)
    return pl.pallas_call(
        crf_kernel,
        name="crf",
        out_shape=jax.ShapeDtypeStruct((cells, bins, states), F32),
        in_specs=[vmem] * 3,
        out_specs=vmem,
        scratch_shapes=[
            pltpu.VMEM((cells, bins, states), F32),
            pltpu.VMEM((cells, states, 2 * states), BF16),
            pltpu.VMEM((cells, states, 2 * states), BF16),
            pltpu.VMEM((cells, 2 * count - 1, states, 2 * states), BF16),
            vec, vec, vec, vec, vec, vec,
            pltpu.VMEM((count * cells, states), F32),
            pltpu.VMEM((count * cells, states), F32),
            pltpu.VMEM((cells, bins, states), F32),
            pltpu.VMEM((cells, bins, states), F32),
            pltpu.SemaphoreType.DMA((2,)),
            pltpu.SemaphoreType.DMA((2,)),
        ],
        compiler_params=pltpu.CompilerParams(
            collective_id=1, has_side_effects=True, vmem_limit_bytes=40 << 20
        ),
    )(features, heads, transitions)


def with_halo(block, sides, width):
    for axis, dim in sides:
        count = lax.axis_size(axis)
        forward = [(i, i + 1) for i in range(count - 1)]
        backward = [(target, source) for source, target in forward]
        low = lax.ppermute(
            lax.slice_in_dim(block, block.shape[dim] - width, None, axis=dim), axis, forward
        )
        high = lax.ppermute(lax.slice_in_dim(block, 0, width, axis=dim), axis, backward)
        block = jnp.concatenate([low, block, high], axis=dim)
    return block


def scaled(values):
    return values * lax.rsqrt(jnp.mean(values * values, axis=-1, keepdims=True) + 1e-06)


def tap_stack(conv_input, spacing_multiplier):
    out_rows = conv_input.shape[0] - 2 * spacing_multiplier
    return jnp.concatenate(
        [
            conv_input[0:out_rows],
            conv_input[spacing_multiplier : spacing_multiplier + out_rows],
            conv_input[2 * spacing_multiplier : 2 * spacing_multiplier + out_rows],
        ],
        axis=1,
    )


def branch(stacked, conv_slice, proj_slice):
    flat_weight = conv_slice.reshape(conv_slice.shape[0], -1)
    conv_out = lax.dot_general(
        stacked, flat_weight, (((1,), (1,)), ((), ())), preferred_element_type=jnp.float32
    )
    hidden = jax.nn.gelu(conv_out).astype(jnp.bfloat16)
    partial_value = jnp.dot(hidden, proj_slice, preferred_element_type=jnp.float32)
    return lax.psum(partial_value.astype(jnp.bfloat16), "cell").astype(jnp.float32)


def per_device(dna_bases, stem_weight, conv_weight, proj_weight, emission_head_weight, transitions):
    bin_rows = dna_bases.shape[0] // BIN_BP
    base_hits = dna_bases.reshape(bin_rows, BIN_BP, 1) == jnp.arange(4, dtype=jnp.int32)
    one_hot = base_hits.astype(jnp.bfloat16).reshape(bin_rows, BIN_BP * 4)
    stem_out = jnp.dot(one_hot, stem_weight, preferred_element_type=jnp.float32).astype(
        jnp.bfloat16
    )
    layers = conv_weight.shape[0]
    residual = stem_out.astype(jnp.float32)
    for layer_position in range(layers):
        spacing_multiplier = BASE_DILATION * 2**layer_position
        conv_input = jax.nn.gelu(scaled(residual)).astype(jnp.bfloat16)
        widened = with_halo(conv_input, (("seq", 0),), spacing_multiplier)
        residual = residual + branch(
            tap_stack(widened, spacing_multiplier),
            conv_weight[layer_position],
            proj_weight[layer_position],
        )
    trunk_features = scaled(residual).astype(jnp.bfloat16)
    return crf(trunk_features, emission_head_weight, transitions)


def solution(mesh):
    placed = (
        P(("groups", "seq")),
        P(),
        P(None, "cell", None, None),
        P(None, "cell", None),
        P("cell", None, None),
        P("cell", None, None),
    )
    return jax.shard_map(
        per_device,
        mesh=mesh,
        in_specs=placed,
        out_specs=P("cell", ("groups", "seq"), None),
        check_vma=False,
    )
```

time: 271 us -> 141 us (0.52)
  matrix products: 104 us -> 3.93 us
  Pallas kernels: 0 us -> 34.2 us
  other arithmetic: 37.8 us -> 4.25 us
  waiting for transfers between devices: 96.8 us -> 67.7 us
    dot_general x114 -> x0, matrix products: 97.2 us -> none  [the longest x56 40 us: block_product(): jnp.einsum('ylv,vu->ylu', running_state, transition_matrix, precision=lax...]
    pallas_call x0 -> x1, Pallas kernels: none -> 34.2 us  [crf(): pl.pallas_call(crf_kernel, name='crf', out_shape=jax.ShapeDtypeStruct((ce...]
    all_gather x1 -> x0, waiting for transfers between devices: 27.8 us -> none  [prefix(): gathered = lax.all_gather(value.astype(jnp.bfloat16), axis)]
    dynamic_update_slice x16 -> x0, other arithmetic: 17.7 us -> none  [per_device(): segment_list, block = lax.map(block_product, (trans_exp, factors))]
    div x44 -> x0, other arithmetic: 11.8 us -> none  [the longest x33 10.7 us: vec_peak(): return vector / jnp.max(vector, axis=-1, keepdims=True)]
    ppermute x2, waiting for transfers between devices: 6.23 us -> 0.01 us  [with_halo(): lax.ppermute(lax.slice_in_dim(block, 0, width, axis=dim), axis, backward)]
    psum x2, waiting for transfers between devices: 62.7 us -> 66.7 us  [branch(): lax.psum(partial_value.astype(jnp.bfloat16), 'cell').astype(jnp.float32)]
  transfers between devices with their start and end apart: 7 -> 6, of which waited for: 5 -> 4; matrix products, arithmetic and copies ran while one was open for 1% -> 1% of each run, Pallas kernels for 0% -> 0%
where the time goes in v1:
time: 141 us; the launch traced here: 140 us
  waiting for transfers between devices  67.7 us (48%)
  Pallas kernels  34.2 us (24%)
  between operations  13.6 us (10%)
  starting transfers between devices  12.9 us (9%)
  other arithmetic  4.25 us (3%)
  matrix products  3.93 us (3%)
  local copies, waits for them, and re-layouts  3.55 us (3%)
    psum x2, waiting for transfers between devices, branch(): lax.psum(partial_value.astype(jnp.bfloat16), 'cell').astype(jnp.float32)  66.7 us
    pallas_call x1, Pallas kernels, crf(): pl.pallas_call(crf_kernel, name='crf', out_shape=jax.ShapeDtypeStruct((ce...  34.2 us
    ppermute x2, starting transfers between devices, with_halo(): lax.ppermute(lax.slice_in_dim(block, block.shape[dim] - width, None, axis...  10.3 us
    dot_general x2, matrix products, branch(): jnp.dot(hidden, proj_slice, preferred_element_type=jnp.float32)  3.4 us
  transfers between devices with their start and end apart: 6, of which 4 were waited for; matrix products, arithmetic and copies ran while one was open for 1% of the time, Pallas kernels for 0%

profile of v1, /device:TPU:0, one launch (start us, length us, event | category | flops | bytes accessed | tf_op | source)
XLA Modules:
  0.0 140.1 jit_solution(2984064753405428009)
XLA Ops:
  6.5 1.0 copy.9
  7.5 0.1 eq.26
  7.7 0.5 multiply_reduce_fusion.2
  8.2 0.2 fusion.25
  8.4 1.3 collective-permute-start.1
  9.7 5.7 %collective-permute-start = (bf16[4,768]{1,0:T(4,128)(2,1)S(1)}, bf16[4,768]{1,0:T(4,128)(2,1)S(1)}, u32[]{:S(2)}, u32[]{:S(2)}) collective-permute-start(bf16[4,768]{1,0:T(4,128)(2,1)S(1)} %get-tuple-element.9), channel_id=1, source_target_pairs={{0,4},{4,8},{8,12},{1,5},{5,9},{9,13},{2,6},{6,10},{10,14},{3,7},{... | collective-permute-start | bytes 18440 | tf_op jit(solution)/shard_map/ppermute | solution.py:274
  15.5 0.1 fusion.87
  15.5 0.4 copy.10
  16.0 0.8 collective-permute-done
  16.8 1.1 convolution_convert_fusion.2
  18.0 34.2 %all-reduce.3.cloned.1.call-done = bf16[64,768]{1,0:T(8,128)(2,1)} async-done(((bf16[64,768]{1,0:T(8,128)(2,1)}), bf16[64,768]{1,0:T(8,128)(2,1)}) %all-reduce.3.cloned.1.call-update) | async-done | bytes 98320 | tf_op jit(solution)/shard_map/psum | solution.py:305
  52.2 1.0 multiply_reduce_fusion.1
  53.2 1.0 fusion.33
  54.2 1.3 collective-permute-start.3
  55.5 4.5 %collective-permute-start.2 = (bf16[8,768]{1,0:T(8,128)(2,1)S(1)}, bf16[8,768]{1,0:T(8,128)(2,1)S(1)}, u32[]{:S(2)}, u32[]{:S(2)}) collective-permute-start(bf16[8,768]{1,0:T(8,128)(2,1)S(1)} %get-tuple-element.7), channel_id=1, source_target_pairs={{0,4},{4,8},{8,12},{1,5},{5,9},{9,13},{2,6},{6,10},{10,14},{3,7},{... | collective-permute-start | bytes 36872 | tf_op jit(solution)/shard_map/ppermute | solution.py:274
  60.1 0.4 copy.11
  60.5 0.8 copy.13
  61.3 0.2 collective-permute-done.2
  61.5 2.3 %convolution_convert_fusion.1 = bf16[64,768]{1,0:T(8,128)(2,1)} fusion(bf16[2,96,768]{2,1,0:T(8,128)(2,1)} %param.9, bf16[96,2304]{1,0:T(8,128)(2,1)} %bitcast.21, bf16[8,768]{1,0:T(8,128)(2,1)S(1)} %collective-permute-done.3, bf16[64,768]{1,0:T(8,128)(2,1)S(1)} %fusion.33, bf16[8,768]{1,0:T(8,128)(2,1)S(1)} %collective-permute-done.2), kind=kOutput, calls=%fused_computation.2 | convolution fusion | flops 39327744 | bytes 811008 | tf_op jit(solution)/shard_map/dot_general | solution.py:304
  63.8 32.5 %all-reduce.5.cloned.1.call-done = bf16[64,768]{1,0:T(8,128)(2,1)} async-done(((bf16[64,768]{1,0:T(8,128)(2,1)}), bf16[64,768]{1,0:T(8,128)(2,1)}) %all-reduce.5.cloned.1.call-update) | async-done | bytes 98320 | tf_op jit(solution)/shard_map/psum | solution.py:305
  96.3 1.0 multiply_reduce_fusion
  97.4 1.0 multiply_convert_fusion.feat_ref
  98.4 34.2 %crf.1 = f32[8,64,128]{2,1,0:T(8,128)S(1)} custom-call(bf16[64,768]{1,0:T(8,128)(2,1)S(1)} %multiply_convert_fusion.feat_ref, bf16[8,768,128]{2,1,0:T(8,128)(2,1)S(1)} %copy-done.1, f32[8,128,128]{2,1,0:T(8,128)S(1)} %copy-done.2), custom_call_target="tpu_custom_call" | custom-call | tf_op jit(solution)/shard_map/crf/pallas_call | solution.py:244
  132.6 0.7 copy.17
  (26 shorter events, 0.2 us)
Async XLA Ops:
  6.5 1.2 copy-start
  6.5 8.9 %copy-start.4 = (bf16[2,96,3,768]{3,1,2,0:T(8,128)(2,1)S(1)}, bf16[2,96,3,768]{3,1,2,0:T(8,128)(2,1)}, u32[]{:S(2)}) copy-start(bf16[2,96,3,768]{3,1,2,0:T(8,128)(2,1)} %param.8) | copy-start | bytes 2654212
  6.5 45.6 %all-reduce.3.cloned.1.call-start = ((), (), s32[]{:S(2)}) async-start(), calls=%async_computation | async-start | bytes 196608 | tf_op jit(solution)/shard_map/psum | solution.py:305
  8.4 7.6 %collective-permute-start.1 = (bf16[4,768]{1,0:T(4,128)(2,1)S(1)}, bf16[4,768]{1,0:T(4,128)(2,1)S(1)}, u32[]{:S(2)}, u32[]{:S(2)}) collective-permute-start(bf16[4,768]{1,0:T(4,128)(2,1)S(1)} %get-tuple-element.10), channel_id=1, source_target_pairs={{4,0},{8,4},{12,8},{5,1},{9,5},{13,9},{6,2},{10,6},{14,10},{7,3},{... | collective-permute-start | bytes 18440 | tf_op jit(solution)/shard_map/ppermute | solution.py:277
  9.7 7.1 %copy-start.5 = (bf16[2,96,768]{2,1,0:T(8,128)(2,1)S(1)}, bf16[2,96,768]{2,1,0:T(8,128)(2,1)}, u32[]{:S(2)}) copy-start(bf16[2,96,768]{2,1,0:T(8,128)(2,1)} %param.9) | copy-start | bytes 884740
  9.7 7.1 %collective-permute-start = (bf16[4,768]{1,0:T(4,128)(2,1)S(1)}, bf16[4,768]{1,0:T(4,128)(2,1)S(1)}, u32[]{:S(2)}, u32[]{:S(2)}) collective-permute-start(bf16[4,768]{1,0:T(4,128)(2,1)S(1)} %get-tuple-element.9), channel_id=1, source_target_pairs={{0,4},{4,8},{8,12},{1,5},{5,9},{9,13},{2,6},{6,10},{10,14},{3,7},{... | collective-permute-start | bytes 18440 | tf_op jit(solution)/shard_map/ppermute | solution.py:274
  17.9 78.4 %all-reduce.5.cloned.1.call-start = ((), (), s32[]{:S(2)}) async-start(), calls=%async_computation.1 | async-start | bytes 196608 | tf_op jit(solution)/shard_map/psum | solution.py:305
  54.2 7.1 %collective-permute-start.3 = (bf16[8,768]{1,0:T(8,128)(2,1)S(1)}, bf16[8,768]{1,0:T(8,128)(2,1)S(1)}, u32[]{:S(2)}, u32[]{:S(2)}) collective-permute-start(bf16[8,768]{1,0:T(8,128)(2,1)S(1)} %get-tuple-element.8), channel_id=1, source_target_pairs={{4,0},{8,4},{12,8},{5,1},{9,5},{13,9},{6,2},{10,6},{14,10},{7,3},{... | collective-permute-start | bytes 36872 | tf_op jit(solution)/shard_map/ppermute | solution.py:277
  55.5 5.9 %collective-permute-start.2 = (bf16[8,768]{1,0:T(8,128)(2,1)S(1)}, bf16[8,768]{1,0:T(8,128)(2,1)S(1)}, u32[]{:S(2)}, u32[]{:S(2)}) collective-permute-start(bf16[8,768]{1,0:T(8,128)(2,1)S(1)} %get-tuple-element.7), channel_id=1, source_target_pairs={{0,4},{4,8},{8,12},{1,5},{5,9},{9,13},{2,6},{6,10},{10,14},{3,7},{... | collective-permute-start | bytes 36872 | tf_op jit(solution)/shard_map/ppermute | solution.py:274
  60.5 35.8 %copy-start.3 = (bf16[64,768]{1,0:T(8,128)(2,1)S(1)}, bf16[64,768]{1,0:T(8,128)(2,1)}, u32[]{:S(2)}) copy-start(bf16[64,768]{1,0:T(8,128)(2,1)} %all-reduce.3.cloned.1.call-done) | copy-start | bytes 294916
  61.3 37.0 %copy-start.1 = (bf16[8,768,128]{2,1,0:T(8,128)(2,1)S(1)}, bf16[8,768,128]{2,1,0:T(8,128)(2,1)}, u32[]{:S(2)}) copy-start(bf16[8,768,128]{2,1,0:T(8,128)(2,1)} %head_ref.1) | copy-start | bytes 4718596
  61.3 37.0 %copy-start.2 = (f32[8,128,128]{2,1,0:T(8,128)S(1)}, f32[8,128,128]{2,1,0:T(8,128)}, u32[]{:S(2)}) copy-start(f32[8,128,128]{2,1,0:T(8,128)} %trans_ref.1) | copy-start | bytes 1572868
Sparse Core Ops, SparseCore 0:
  18.1 34.0 all-reduce.2
  63.9 32.3 all-reduce.4

commit v2 on v1

--- a/solution.py
+++ b/solution.py
@@ -10,6 +10,7 @@
 BIN_BP = 128
 BASE_DILATION = 4
 SUB = 8
+HALO = 16
 MESH = pl.DeviceIdType.MESH
 F32 = jnp.float32
 BF16 = jnp.bfloat16
@@ -57,39 +58,180 @@
     return jnp.max(jnp.max(x, axis=-1, keepdims=True), axis=-2, keepdims=True)
 
 
+def rms(v):
+    return v * lax.rsqrt(jnp.mean(v * v, axis=-1, keepdims=True) + 1e-06)
+
+
 def crf_kernel(
-    feat_ref, head_ref, trans_ref, out_ref,
-    f_ref, pair_ref, flip_ref, tree_ref, vin, win, vgot, wgot, vout, wout, st_ref, af_ref,
-    al_ref, be_ref, ssem, rsem,
+    bases_ref, stem_hbm, conv_hbm, proj_ref, head_hbm, trans_ref, out_ref,
+    stem_ref, conv_ref, head_ref, lsem,
+    wide_ref, wts_ref, gath_ref, hs_sem, hr_sem, ws_sem, wr_sem, gs_sem, gr_sem, feat_ref,
+    f_ref, trn_ref, pair_ref, flip_ref, tree_ref, vin, win, vgot, wgot, vout, wout, st_ref,
+    af_ref, al_ref, be_ref, ssem, rsem,
 ):
     cells, states = head_ref.shape[0], head_ref.shape[2]
     bins = feat_ref.shape[0]
     count = bins // SUB
+    layers = conv_ref.shape[0]
+    rows_wide = bins + 2 * HALO
     n = lax.axis_size("seq")
     me = lax.axis_index("seq")
-
-    if n > 1:
-        barrier = pltpu.get_barrier_semaphore()
-
-        @pl.when(me > 0)
-        def _():
-            pl.semaphore_signal(barrier, inc=1, device_id={"seq": me - 1}, device_id_type=MESH)
-
-        @pl.when(me < n - 1)
-        def _():
-            pl.semaphore_signal(barrier, inc=1, device_id={"seq": me + 1}, device_id_type=MESH)
-
-        inner = jnp.logical_and(me > 0, me < n - 1)
-        pl.semaphore_wait(barrier, jnp.where(inner, 2, 1))
+    cell = lax.axis_index("cell")
+    near = cell + 1 - 2 * (cell % 2)
+    far = (cell + 2) % 4
+    diag = (near + 2) % 4
+    peers = (None, near, far, diag)
+
+    loads = [
+        pltpu.make_async_copy(src, dst, lsem.at[i])
+        for i, (src, dst) in enumerate(
+            [(stem_hbm, stem_ref), (conv_hbm, conv_ref), (head_hbm, head_ref)]
+        )
+    ]
+    for load in loads:
+        load.start()
+
+    barrier = pltpu.get_barrier_semaphore()
+    for peer in peers[1:]:
+        pl.semaphore_signal(barrier, inc=1, device_id={"cell": peer}, device_id_type=MESH)
+
+    @pl.when(me > 0)
+    def _():
+        pl.semaphore_signal(barrier, inc=1, device_id={"seq": me - 1}, device_id_type=MESH)
+
+    @pl.when(me < n - 1)
+    def _():
+        pl.semaphore_signal(barrier, inc=1, device_id={"seq": me + 1}, device_id_type=MESH)
+
+    inner = jnp.logical_and(me > 0, me < n - 1)
+    pl.semaphore_wait(barrier, jnp.where(inner, 5, 4 if n > 1 else 3))
+
+    upward = pltpu.make_async_remote_copy(
+        bases_ref.at[pl.ds(bins - HALO, HALO)], wide_ref.at[pl.ds(0, HALO)],
+        hs_sem.at[0], hr_sem.at[0],
+        device_id={"seq": jnp.minimum(me + 1, n - 1)}, device_id_type=MESH,
+    )
+    downward = pltpu.make_async_remote_copy(
+        bases_ref.at[pl.ds(0, HALO)], wide_ref.at[pl.ds(HALO, HALO)],
+        hs_sem.at[1], hr_sem.at[1],
+        device_id={"seq": jnp.maximum(me - 1, 0)}, device_id_type=MESH,
+    )
+
+    @pl.when(me < n - 1)
+    def _():
+        upward.start()
+
+    @pl.when(me > 0)
+    def _():
+        downward.start()
+
+    def send_weight(layer, k):
+        own = pl.ds(0, proj_ref.shape[1])
+        source = wts_ref.at[layer, 2, own] if k == 3 else proj_ref.at[layer]
+        return pltpu.make_async_remote_copy(
+            source, wts_ref.at[layer, k, own], ws_sem.at[layer, k], wr_sem.at[layer, k],
+            device_id={"cell": far if k == 2 else near}, device_id_type=MESH,
+        )
+
+    def send_hidden(layer, k):
+        return pltpu.make_async_remote_copy(
+            gath_ref.at[layer, 0], gath_ref.at[layer, k], gs_sem.at[layer, k],
+            gr_sem.at[layer, k], device_id={"cell": peers[k]}, device_id_type=MESH,
+        )
+
+    for layer in range(layers):
+        send_weight(layer, 2).start()
+        send_weight(layer, 1).start()
+    held, padded = proj_ref.shape[1], wts_ref.shape[2]
+    for layer in range(layers):
+        wts_ref[layer, 0, pl.ds(0, held), :] = proj_ref[layer]
+        if padded > held:
+            for k in range(4):
+                wts_ref[layer, k, pl.ds(held, padded - held), :] = jnp.zeros(
+                    (padded - held, wts_ref.shape[3]), BF16
+                )
+
+    def prepare(c, _):
+        raw = trans_ref[c]
+        t = jnp.exp(raw - top(raw))
+        trn_ref[c] = t
+        pair_ref[c] = beside(t)
+        flip_ref[c] = beside(t.T)
+        return 0
+
+    lax.fori_loop(0, cells // 2, prepare, 0)
+
+    columns = lax.broadcasted_iota(jnp.int32, (BIN_BP, 4 * BIN_BP), 1)
+    spread = (columns // 4 == lax.broadcasted_iota(jnp.int32, columns.shape, 0)).astype(BF16)
+
+    @pl.when(me > 0)
+    def _():
+        upward.wait_recv()
+
+    @pl.when(me == 0)
+    def _():
+        wide_ref[pl.ds(0, HALO), :] = jnp.zeros((HALO, BIN_BP), jnp.int32)
+
+    @pl.when(me < n - 1)
+    def _():
+        downward.wait_recv()
+
+    @pl.when(me == n - 1)
+    def _():
+        wide_ref[pl.ds(HALO, HALO), :] = jnp.zeros((HALO, BIN_BP), jnp.int32)
+
+    bases = jnp.concatenate(
+        [wide_ref[pl.ds(0, HALO), :], bases_ref[...], wide_ref[pl.ds(HALO, HALO), :]], axis=0
+    )
+    repeated = jnp.dot(
+        bases.astype(F32).astype(BF16), spread, preferred_element_type=F32
+    )
+    which = (lax.broadcasted_iota(jnp.int32, repeated.shape, 1) % 4).astype(F32)
+    one_hot = jnp.where(repeated == which, 1.0, 0.0).astype(BF16)
+    loads[0].wait()
+    residual = jnp.dot(one_hot, stem_ref[...], preferred_element_type=F32).astype(BF16).astype(F32)
+    place = lax.broadcasted_iota(jnp.int32, residual.shape, 0) + (me * bins - HALO)
+    inside = jnp.logical_and(place >= 0, place < n * bins)
+    loads[1].wait()
+    for layer in range(layers):
+        dilation = BASE_DILATION * 2**layer
+        conv_in = jnp.where(inside, jax.nn.gelu(rms(residual)), 0.0).astype(BF16)
+        taps = [
+            lax.dot_general(
+                conv_in, conv_ref[layer, k], (((1,), (1,)), ((), ())), preferred_element_type=F32
+            )
+            for k in range(3)
+        ]
+        conv_out = (
+            pltpu.roll(taps[0], dilation, 0)
+            + taps[1]
+            + pltpu.roll(taps[2], rows_wide - dilation, 0)
+        )
+        gath_ref[layer, 0] = jax.nn.gelu(conv_out).astype(BF16)
+        for k in (2, 3, 1):
+            send_hidden(layer, k).start()
+        send_weight(layer, 2).wait_recv()
+        send_weight(layer, 3).start()
+        if layer == 0:
+            lax.fori_loop(cells // 2, cells, prepare, 0)
+        for k in (1, 2, 3):
+            if k != 2:
+                send_weight(layer, k).wait_recv()
+            send_hidden(layer, k).wait_recv()
+        hidden = jnp.concatenate([gath_ref[layer, k] for k in range(4)], axis=1)
+        residual = residual + jnp.dot(
+            hidden,
+            wts_ref[layer].reshape(4 * padded, wts_ref.shape[3]),
+            preferred_element_type=F32,
+        )
+    feat_ref[...] = rms(residual[HALO : HALO + bins]).astype(BF16)
+    loads[2].wait()
 
     def chain(c, _):
         scores = jnp.dot(feat_ref[...], head_ref[c], preferred_element_type=F32)
         f_ref[c] = jnp.exp(scores - jnp.max(scores, axis=1, keepdims=True))
-        raw = trans_ref[c]
-        t = jnp.exp(raw - top(raw))
-        pair = beside(t)
-        pair_ref[c] = pair
-        flip_ref[c] = beside(t.T)
+        t = trn_ref[c]
+        pair = pair_ref[c]
         twice = jnp.concatenate([pair, pair], axis=0)
         x = t[None] * f_ref[c, pl.ds(0, count, stride=SUB), :][:, None, :]
         for j in range(1, SUB):
@@ -234,21 +376,51 @@
                 wout, wgot, ssem.at[1], rsem.at[1], device_id={"seq": me - 1}, device_id_type=MESH
             ).wait_send()
 
-
-def crf(features, heads, transitions):
-    bins = features.shape[0]
-    cells, _, states = heads.shape
+    @pl.when(me < n - 1)
+    def _():
+        upward.wait_send()
+
+    @pl.when(me > 0)
+    def _():
+        downward.wait_send()
+
+    for layer in range(layers):
+        for k in (1, 2, 3):
+            send_weight(layer, k).wait_send()
+            send_hidden(layer, k).wait_send()
+
+
+def per_device(dna_bases, stem_weight, conv_weight, proj_weight, emission_head_weight, transitions):
+    bins = dna_bases.shape[0] // BIN_BP
+    cells, _, states = emission_head_weight.shape
+    layers, held, taps, wide = conv_weight.shape
+    inner = pl.cdiv(held, 128) * 128
     count = bins // SUB
+    assert HALO >= BASE_DILATION * (2**layers - 1) and lax.axis_size("cell") == 4
+    rows = bins + 2 * HALO
     vmem = pl.BlockSpec(memory_space=pltpu.VMEM)
+    hbm = pl.BlockSpec(memory_space=pl.ANY)
     vec = pltpu.VMEM((cells, states), F32)
+    dma = pltpu.SemaphoreType.DMA
     return pl.pallas_call(
         crf_kernel,
         name="crf",
         out_shape=jax.ShapeDtypeStruct((cells, bins, states), F32),
-        in_specs=[vmem] * 3,
+        in_specs=[vmem, hbm, hbm, vmem, hbm, vmem],
         out_specs=vmem,
         scratch_shapes=[
+            pltpu.VMEM(stem_weight.shape, BF16),
+            pltpu.VMEM((layers, taps, inner, wide), BF16),
+            pltpu.VMEM(emission_head_weight.shape, BF16),
+            dma((3,)),
+            pltpu.VMEM((2 * HALO, BIN_BP), jnp.int32),
+            pltpu.VMEM((layers, 4, inner, wide), BF16),
+            pltpu.VMEM((layers, 4, rows, inner), BF16),
+            dma((2,)), dma((2,)),
+            dma((layers, 4)), dma((layers, 4)), dma((layers, 4)), dma((layers, 4)),
+            pltpu.VMEM((bins, wide), BF16),
             pltpu.VMEM((cells, bins, states), F32),
+            pltpu.VMEM((cells, states, states), F32),
             pltpu.VMEM((cells, states, 2 * states), BF16),
             pltpu.VMEM((cells, states, 2 * states), BF16),
             pltpu.VMEM((cells, 2 * count - 1, states, 2 * states), BF16),
@@ -257,74 +429,19 @@
             pltpu.VMEM((count * cells, states), F32),
             pltpu.VMEM((cells, bins, states), F32),
             pltpu.VMEM((cells, bins, states), F32),
-            pltpu.SemaphoreType.DMA((2,)),
-            pltpu.SemaphoreType.DMA((2,)),
+            dma((2,)), dma((2,)),
         ],
         compiler_params=pltpu.CompilerParams(
-            collective_id=1, has_side_effects=True, vmem_limit_bytes=40 << 20
+            collective_id=1, has_side_effects=True, vmem_limit_bytes=48 << 20
         ),
-    )(features, heads, transitions)
-
-
-def with_halo(block, sides, width):
-    for axis, dim in sides:
-        count = lax.axis_size(axis)
-        forward = [(i, i + 1) for i in range(count - 1)]
-        backward = [(target, source) for source, target in forward]
-        low = lax.ppermute(
-            lax.slice_in_dim(block, block.shape[dim] - width, None, axis=dim), axis, forward
-        )
-        high = lax.ppermute(lax.slice_in_dim(block, 0, width, axis=dim), axis, backward)
-        block = jnp.concatenate([low, block, high], axis=dim)
-    return block
-
-
-def scaled(values):
-    return values * lax.rsqrt(jnp.mean(values * values, axis=-1, keepdims=True) + 1e-06)
-
-
-def tap_stack(conv_input, spacing_multiplier):
-    out_rows = conv_input.shape[0] - 2 * spacing_multiplier
-    return jnp.concatenate(
-        [
-            conv_input[0:out_rows],
-            conv_input[spacing_multiplier : spacing_multiplier + out_rows],
-            conv_input[2 * spacing_multiplier : 2 * spacing_multiplier + out_rows],
-        ],
-        axis=1,
-    )
-
-
-def branch(stacked, conv_slice, proj_slice):
-    flat_weight = conv_slice.reshape(conv_slice.shape[0], -1)
-    conv_out = lax.dot_general(
-        stacked, flat_weight, (((1,), (1,)), ((), ())), preferred_element_type=jnp.float32
-    )
-    hidden = jax.nn.gelu(conv_out).astype(jnp.bfloat16)
-    partial_value = jnp.dot(hidden, proj_slice, preferred_element_type=jnp.float32)
-    return lax.psum(partial_value.astype(jnp.bfloat16), "cell").astype(jnp.float32)
-
-
-def per_device(dna_bases, stem_weight, conv_weight, proj_weight, emission_head_weight, transitions):
-    bin_rows = dna_bases.shape[0] // BIN_BP
-    base_hits = dna_bases.reshape(bin_rows, BIN_BP, 1) == jnp.arange(4, dtype=jnp.int32)
-    one_hot = base_hits.astype(jnp.bfloat16).reshape(bin_rows, BIN_BP * 4)
-    stem_out = jnp.dot(one_hot, stem_weight, preferred_element_type=jnp.float32).astype(
-        jnp.bfloat16
-    )
-    layers = conv_weight.shape[0]
-    residual = stem_out.astype(jnp.float32)
-    for layer_position in range(layers):
-        spacing_multiplier = BASE_DILATION * 2**layer_position
-        conv_input = jax.nn.gelu(scaled(residual)).astype(jnp.bfloat16)
-        widened = with_halo(conv_input, (("seq", 0),), spacing_multiplier)
-        residual = residual + branch(
-            tap_stack(widened, spacing_multiplier),
-            conv_weight[layer_position],
-            proj_weight[layer_position],
-        )
-    trunk_features = scaled(residual).astype(jnp.bfloat16)
-    return crf(trunk_features, emission_head_weight, transitions)
+    )(
+        dna_bases.reshape(bins, BIN_BP),
+        stem_weight,
+        jnp.pad(conv_weight.transpose(0, 2, 1, 3), ((0, 0), (0, 0), (0, inner - held), (0, 0))),
+        proj_weight,
+        emission_head_weight,
+        transitions,
+    )
 
 
 def solution(mesh):

time: 141 us -> 55.3 us (0.39)
  waiting for transfers between devices: 67.7 us -> 0 us
  Pallas kernels: 34.2 us -> 50.4 us
  between operations: 13.6 us -> 0.02 us
  starting transfers between devices: 12.9 us -> 0 us
  other arithmetic: 4.25 us -> 0 us
  matrix products: 3.93 us -> 0 us
    psum x2 -> x0, waiting for transfers between devices: 66.7 us -> none  [branch(): lax.psum(partial_value.astype(jnp.bfloat16), 'cell').astype(jnp.float32)]
    pallas_call x1, Pallas kernels: 34.2 us -> 50.4 us  [per_device(): pl.pallas_call(crf_kernel, name='crf', out_shape=jax.ShapeDtypeStruct((ce...]
    ppermute x4 -> x0, starting transfers between devices: 12.8 us -> none  [the longest x2 10.3 us: with_halo(): lax.ppermute(lax.slice_in_dim(block, block.shape[dim] - width, None, axis...]
    dot_general x3 -> x0, matrix products: 3.93 us -> none  [the longest x2 3.4 us: branch(): jnp.dot(hidden, proj_slice, preferred_element_type=jnp.float32)]
    convert_element_type x3 -> x0, other arithmetic: 2.18 us -> none  [the longest x2 1.2 us: per_device(): conv_input = jax.nn.gelu(scaled(residual)).astype(jnp.bfloat16)]
    reduce_sum x2 -> x0, other arithmetic: 2.05 us -> none  [scaled(): jnp.mean(values * values, axis=-1, keepdims=True) + 1e-06]
    unnamed x15 -> x11, local copies, waits for them, and re-layouts: 1.58 us -> 3.19 us
  transfers between devices with their start and end apart: 6 -> 0, of which waited for: 4 -> 0; matrix products, arithmetic and copies ran while one was open for 1% -> 0% of each run, Pallas kernels for 0% -> 0%
where the time goes in v2:
time: 55.3 us; the launch traced here: 55 us
  Pallas kernels  50.4 us (91%)
  local copies, waits for them, and re-layouts  4.57 us (8%)
    pallas_call x1, Pallas kernels, per_device(): pl.pallas_call(crf_kernel, name='crf', out_shape=jax.ShapeDtypeStruct((ce...  50.4 us
    unnamed x11, local copies, waits for them, and re-layouts  3.19 us
    pad x1, local copies, waits for them, and re-layouts, per_device(): jnp.pad(conv_weight.transpose(0, 2, 1, 3), ((0, 0), (0, 0), (0, inner - h...  1.38 us

profile of v2, /device:TPU:0, one launch (start us, length us, event | category | flops | bytes accessed | tf_op | source)
XLA Modules:
  0.0 55.0 jit_solution(5733874200856796844)
XLA Ops:
  0.0 0.0 copy-start
  0.0 0.0 copy-start.3
  0.0 0.0 copy-start.4
  0.0 1.4 %pad.4.conv_hbm = bf16[2,3,128,768]{3,2,1,0:T(8,128)(2,1)S(1)} pad(bf16[2,3,96,768]{3,2,1,0:T(8,128)(2,1)} %bitcast.3, bf16[]{:T(256)} %constant.2.clone.1), padding=0_0x0_0x0_32x0_0 | pad | bytes 2064386 | tf_op jit(solution)/shard_map/jit(_pad)/pad | solution.py:440
  1.4 0.3 copy-done
  1.7 0.0 copy-done.3
  1.7 0.0 copy-done.4
  1.7 0.0 copy-start.1
  1.7 1.1 %copy-done.1 = bf16[512,768]{1,0:T(8,128)(2,1)S(1)} copy-done((bf16[512,768]{1,0:T(8,128)(2,1)S(1)}, bf16[512,768]{1,0:T(8,128)(2,1)}, u32[]{:S(2)}) %copy-start.1) | copy-done | bytes 786456
  2.8 0.0 copy-start.2
  2.8 1.0 %copy-done.2 = f32[8,128,128]{2,1,0:T(8,128)S(1)} copy-done((f32[8,128,128]{2,1,0:T(8,128)S(1)}, f32[8,128,128]{2,1,0:T(8,128)}, u32[]{:S(2)}) %copy-start.2) | copy-done | bytes 524312
  3.9 50.4 %crf.1 = f32[8,64,128]{2,1,0:T(8,128)S(1)} custom-call(s32[64,128]{1,0:T(8,128)S(1)} %bitcast.2, bf16[512,768]{1,0:T(8,128)(2,1)S(1)} %copy-done.1, bf16[2,3,128,768]{3,2,1,0:T(8,128)(2,1)S(1)} %pad.4.conv_hbm, bf16[2,96,768]{2,1,0:T(8,128)(2,1)S(1)} %copy-done.3, bf16[8,768,128]{2,1,0:T(8,128)(2,1)S(1)} %copy-done, f32[8,128,128]{2,1,0:T(8,128)S(1)} %copy-done.2), custom_call_target="tpu_custom_call" | custom-call | tf_op jit(solution)/shard_map/crf/pallas_call | solution.py:405
  54.3 0.7 %copy.8 = f32[8,64,128]{2,1,0:T(8,128)} copy(f32[8,64,128]{2,1,0:T(8,128)S(1)} %crf.1) | data formatting | bytes 524288
Async XLA Ops:
  0.0 1.7 %copy-start = (bf16[8,768,128]{2,1,0:T(8,128)(2,1)S(1)}, bf16[8,768,128]{2,1,0:T(8,128)(2,1)}, u32[]{:S(2)}) copy-start(bf16[8,768,128]{2,1,0:T(8,128)(2,1)} %head_hbm.1) | copy-start | bytes 4718596
  0.0 1.7 %copy-start.3 = (bf16[2,96,768]{2,1,0:T(8,128)(2,1)S(1)}, bf16[2,96,768]{2,1,0:T(8,128)(2,1)}, u32[]{:S(2)}) copy-start(bf16[2,96,768]{2,1,0:T(8,128)(2,1)} %proj_ref.1) | copy-start | bytes 884740
  0.0 1.7 %copy-start.4 = (s32[8192]{0:T(1024)S(1)}, s32[8192]{0:T(1024)}, u32[]{:S(2)}) copy-start(s32[8192]{0:T(1024)} %param.6) | copy-start | bytes 98308
  1.7 1.1 %copy-start.1 = (bf16[512,768]{1,0:T(8,128)(2,1)S(1)}, bf16[512,768]{1,0:T(8,128)(2,1)}, u32[]{:S(2)}) copy-start(bf16[512,768]{1,0:T(8,128)(2,1)} %stem_hbm.1) | copy-start | bytes 2359300
  2.8 1.0 %copy-start.2 = (f32[8,128,128]{2,1,0:T(8,128)S(1)}, f32[8,128,128]{2,1,0:T(8,128)}, u32[]{:S(2)}) copy-start(f32[8,128,128]{2,1,0:T(8,128)} %trans_ref.1) | copy-start | bytes 1572868

commit v3 on v2

--- a/solution.py
+++ b/solution.py
@@ -11,6 +11,7 @@
 BASE_DILATION = 4
 SUB = 8
 HALO = 16
+WIDTH = 4
 MESH = pl.DeviceIdType.MESH
 F32 = jnp.float32
 BF16 = jnp.bfloat16
@@ -227,40 +228,50 @@
     feat_ref[...] = rms(residual[HALO : HALO + bins]).astype(BF16)
     loads[2].wait()
 
-    def chain(c, _):
-        scores = jnp.dot(feat_ref[...], head_ref[c], preferred_element_type=F32)
-        f_ref[c] = jnp.exp(scores - jnp.max(scores, axis=1, keepdims=True))
-        t = trn_ref[c]
-        pair = pair_ref[c]
-        twice = jnp.concatenate([pair, pair], axis=0)
-        x = t[None] * f_ref[c, pl.ds(0, count, stride=SUB), :][:, None, :]
+    def chain(i, _):
+        group = [WIDTH * i + k for k in range(WIDTH)]
+        scores = [jnp.dot(feat_ref[...], head_ref[c], preferred_element_type=F32) for c in group]
+        for c, e in zip(group, scores):
+            f_ref[c] = jnp.exp(e - jnp.max(e, axis=1, keepdims=True))
+        twice = [jnp.concatenate([pair_ref[c], pair_ref[c]], axis=0) for c in group]
+        xs = [
+            trn_ref[c][None] * f_ref[c, pl.ds(0, count, stride=SUB), :][:, None, :] for c in group
+        ]
         for j in range(1, SUB):
-            scale = 1.0 / top(x)
-            g = f_ref[c, pl.ds(j, count, stride=SUB), :][:, None, :] * scale
-            y = jnp.dot(
-                beside(x.reshape(count * states, states)), twice, preferred_element_type=F32
-            )
-            x = (y[:, :states] + y[:, states:]).reshape(count, states, states) * g
-        x = x * (1.0 / top(x))
-        nodes = []
-        for k in range(count):
-            nodes.append(beside(x[k]))
-            tree_ref[c, k] = nodes[k]
+            for p, c in enumerate(group):
+                x = xs[p]
+                scale = 1.0 / top(x)
+                g = f_ref[c, pl.ds(j, count, stride=SUB), :][:, None, :] * scale
+                y = jnp.dot(
+                    beside(x.reshape(count * states, states)),
+                    twice[p],
+                    preferred_element_type=F32,
+                )
+                xs[p] = (y[:, :states] + y[:, states:]).reshape(count, states, states) * g
+        layers_of = []
+        for p, c in enumerate(group):
+            x = xs[p] * (1.0 / top(xs[p]))
+            layers_of.append([beside(x[k]) for k in range(count)])
+            for k in range(count):
+                tree_ref[c, k] = layers_of[p][k]
         place = count
-        while len(nodes) > 1:
-            joined = []
-            for k in range(0, len(nodes), 2):
-                right = jnp.concatenate([nodes[k + 1], nodes[k + 1]], axis=0)
-                y = jnp.dot(nodes[k], right, preferred_element_type=F32)
-                y = y[:, :states] + y[:, states:]
-                node = beside(y * (1.0 / top(y)))
-                tree_ref[c, place] = node
-                place += 1
-                joined.append(node)
-            nodes = joined
+        while len(layers_of[0]) > 1:
+            half = len(layers_of[0]) // 2
+            for p, c in enumerate(group):
+                nodes = layers_of[p]
+                joined = []
+                for k in range(half):
+                    right = jnp.concatenate([nodes[2 * k + 1], nodes[2 * k + 1]], axis=0)
+                    y = jnp.dot(nodes[2 * k], right, preferred_element_type=F32)
+                    y = y[:, :states] + y[:, states:]
+                    node = beside(y * (1.0 / top(y)))
+                    tree_ref[c, place + k] = node
+                    joined.append(node)
+                layers_of[p] = joined
+            place += half
         return 0
 
-    lax.fori_loop(0, cells, chain, 0)
+    lax.fori_loop(0, cells // WIDTH, chain, 0)
 
     rows = lax.broadcasted_iota(jnp.int32, (cells, states), 0)
 

time: 55.3 us -> 47.6 us (0.86)
  Pallas kernels: 50.4 us -> 42.8 us
    pallas_call x1, Pallas kernels: 50.4 us -> 42.8 us  [per_device(): pl.pallas_call(crf_kernel, name='crf', out_shape=jax.ShapeDtypeStruct((ce...]
where the time goes in v3:
time: 47.6 us; the launch traced here: 47.3 us
  Pallas kernels  42.8 us (90%)
  local copies, waits for them, and re-layouts  4.57 us (10%)
    pallas_call x1, Pallas kernels, per_device(): pl.pallas_call(crf_kernel, name='crf', out_shape=jax.ShapeDtypeStruct((ce...  42.8 us
    unnamed x11, local copies, waits for them, and re-layouts  3.19 us
    pad x1, local copies, waits for them, and re-layouts, per_device(): jnp.pad(conv_weight.transpose(0, 2, 1, 3), ((0, 0), (0, 0), (0, inner - h...  1.38 us

profile of v3, /device:TPU:0, one launch (start us, length us, event | category | flops | bytes accessed | tf_op | source)
XLA Modules:
  0.0 47.3 jit_solution(9900722445373418518)
XLA Ops:
  0.0 0.0 copy-start
  0.0 0.0 copy-start.3
  0.0 0.0 copy-start.4
  0.0 1.4 %pad.4.conv_hbm = bf16[2,3,128,768]{3,2,1,0:T(8,128)(2,1)S(1)} pad(bf16[2,3,96,768]{3,2,1,0:T(8,128)(2,1)} %bitcast.3, bf16[]{:T(256)} %constant.2.clone.1), padding=0_0x0_0x0_32x0_0 | pad | bytes 2064386 | tf_op jit(solution)/shard_map/jit(_pad)/pad | solution.py:451
  1.4 0.3 copy-done
  1.7 0.0 copy-done.3
  1.7 0.0 copy-done.4
  1.7 0.0 copy-start.1
  1.7 1.1 %copy-done.1 = bf16[512,768]{1,0:T(8,128)(2,1)S(1)} copy-done((bf16[512,768]{1,0:T(8,128)(2,1)S(1)}, bf16[512,768]{1,0:T(8,128)(2,1)}, u32[]{:S(2)}) %copy-start.1) | copy-done | bytes 786456
  2.8 0.0 copy-start.2
  2.8 1.0 %copy-done.2 = f32[8,128,128]{2,1,0:T(8,128)S(1)} copy-done((f32[8,128,128]{2,1,0:T(8,128)S(1)}, f32[8,128,128]{2,1,0:T(8,128)}, u32[]{:S(2)}) %copy-start.2) | copy-done | bytes 524312
  3.9 42.8 %crf.1 = f32[8,64,128]{2,1,0:T(8,128)S(1)} custom-call(s32[64,128]{1,0:T(8,128)S(1)} %bitcast.2, bf16[512,768]{1,0:T(8,128)(2,1)S(1)} %copy-done.1, bf16[2,3,128,768]{3,2,1,0:T(8,128)(2,1)S(1)} %pad.4.conv_hbm, bf16[2,96,768]{2,1,0:T(8,128)(2,1)S(1)} %copy-done.3, bf16[8,768,128]{2,1,0:T(8,128)(2,1)S(1)} %copy-done, f32[8,128,128]{2,1,0:T(8,128)S(1)} %copy-done.2), custom_call_target="tpu_custom_call" | custom-call | tf_op jit(solution)/shard_map/crf/pallas_call | solution.py:416
  46.6 0.7 %copy.8 = f32[8,64,128]{2,1,0:T(8,128)} copy(f32[8,64,128]{2,1,0:T(8,128)S(1)} %crf.1) | data formatting | bytes 524288
Async XLA Ops:
  0.0 1.7 %copy-start = (bf16[8,768,128]{2,1,0:T(8,128)(2,1)S(1)}, bf16[8,768,128]{2,1,0:T(8,128)(2,1)}, u32[]{:S(2)}) copy-start(bf16[8,768,128]{2,1,0:T(8,128)(2,1)} %head_hbm.1) | copy-start | bytes 4718596
  0.0 1.7 %copy-start.3 = (bf16[2,96,768]{2,1,0:T(8,128)(2,1)S(1)}, bf16[2,96,768]{2,1,0:T(8,128)(2,1)}, u32[]{:S(2)}) copy-start(bf16[2,96,768]{2,1,0:T(8,128)(2,1)} %proj_ref.1) | copy-start | bytes 884740
  0.0 1.7 %copy-start.4 = (s32[8192]{0:T(1024)S(1)}, s32[8192]{0:T(1024)}, u32[]{:S(2)}) copy-start(s32[8192]{0:T(1024)} %param.6) | copy-start | bytes 98308
  1.7 1.1 %copy-start.1 = (bf16[512,768]{1,0:T(8,128)(2,1)S(1)}, bf16[512,768]{1,0:T(8,128)(2,1)}, u32[]{:S(2)}) copy-start(bf16[512,768]{1,0:T(8,128)(2,1)} %stem_hbm.1) | copy-start | bytes 2359300
  2.8 1.0 %copy-start.2 = (f32[8,128,128]{2,1,0:T(8,128)S(1)}, f32[8,128,128]{2,1,0:T(8,128)}, u32[]{:S(2)}) copy-start(f32[8,128,128]{2,1,0:T(8,128)} %trans_ref.1) | copy-start | bytes 1572868
